TPU v7x, 32 devices: a whole 2x2x4 slice. The times are simulated.
32 devices in a mesh: band: 8 (over z, x), quarter: 4 (over y, core).
Axes of the slice: x: 2, y: 2, z: 4, core: 2. Of those that a mesh axis runs over, the one named last changes fastest.
Arguments:
- voltages: bfloat16 [32, 2, 524288], P('band', None, 'quarter'), may hold values from -6 to 6
- flagged: int32 [32], P('band'), may hold values 0 or 1
- antenna_source_lookup: int32 [32], replicated, may hold values from 0 to 31, each once
Outputs:
- visibility: bfloat16 [2, 16, 64, 64], P(None, 'band', 'quarter')
Inputs may be any that keep to these rules, and one draw needn't show every extreme that they name: `antenna_source_lookup`: every input antenna appears exactly once.
All inputs are finite; a program needn't handle non-finite values. No bound on the sum of `flagged` on one device may be relied on, other than what follows from the above.
Results may differ from a plain program's by a relative error of at most 0.0074.
Values may be sent and summed in bfloat16 or wider, within the bound.
A program may use at most 64 MiB of HBM per device.

v0:
```python
import math
import jax
import jax.numpy as jnp
from jax import lax
from jax.sharding import PartitionSpec as P

FRAME = 8192
TAPS = 4
CH_DEV = 2


def passed_along(shard, axis, by):
    count = lax.axis_size(axis)
    pairs = [(i, i + by) for i in range(count) if 0 <= i + by < count]
    return lax.ppermute(shard, axis, pairs)


def pfb_window():
    sample_pos = jnp.arange(TAPS * FRAME, dtype=jnp.float32) + 0.5
    offset_units = sample_pos / FRAME - TAPS / 2.0
    hann_taper = 0.5 - 0.5 * jnp.cos(sample_pos * (2.0 * math.pi / (TAPS * FRAME)))
    return (jnp.sinc(offset_units) * hann_taper).reshape(TAPS, FRAME)


def dft_rows(channels):
    bins = jnp.arange(channels, dtype=jnp.int32) + FRAME // 8
    sample_index = jnp.arange(FRAME, dtype=jnp.int32)
    phase_steps = bins[:, None] * sample_index[None, :] % FRAME
    angles = phase_steps.astype(jnp.float32) * (2.0 * math.pi / FRAME)
    stacked = jnp.stack([jnp.cos(angles), -jnp.sin(angles)], axis=1)
    return stacked.reshape(2 * channels, FRAME).astype(jnp.bfloat16)


def left_side(own_rows):
    real_part = own_rows[:, 0]
    imag_part = own_rows[:, 1]
    first = jnp.concatenate([real_part, imag_part], axis=1)
    second = jnp.concatenate([imag_part, -real_part], axis=1)
    return jnp.stack([first, second], axis=1)


def pair_product(left_rows, other_rows):
    right_side = jnp.concatenate([other_rows[:, 0], other_rows[:, 1]], axis=1)
    return jnp.einsum("coki,ckj->ocij", left_rows, right_side, preferred_element_type=jnp.float32)


def table_product(table_rows, windowed_rows):
    return lax.dot_general(
        table_rows, windowed_rows, (((1,), (1,)), ((), ())), preferred_element_type=jnp.float32
    )


def shards(voltages, flagged, antenna_source_lookup):
    antenna_per_device, polarization_count, device_local_samples = voltages.shape
    band_count = lax.axis_size("band")
    quarters = lax.axis_size("quarter")
    spec_dev = device_local_samples // FRAME
    device_signals = antenna_per_device * polarization_count
    keep_mask = (1 - flagged).astype(jnp.bfloat16)
    frames = (voltages * keep_mask[:, None, None]).reshape(device_signals, spec_dev, FRAME)
    window = pfb_window()
    channels = CH_DEV * band_count
    dft_table = dft_rows(channels)
    edge = TAPS - 1
    following = passed_along(frames[:, :edge], "quarter", -1)
    extended = jnp.concatenate([frames, following], axis=1)
    columns = device_signals * spec_dev
    tap_rows = []
    for tap_index in range(TAPS):
        tap_win = (
            window[tap_index] * extended[:, tap_index : tap_index + spec_dev].astype(jnp.float32)
        ).astype(jnp.bfloat16)
        tap_rows.append(tap_win.reshape(columns, FRAME))
    inv_root = 1.0 / math.sqrt(FRAME)
    result = table_product(dft_table, tap_rows[0])
    for tap_index in range(1, TAPS):
        result = result + table_product(dft_table, tap_rows[tap_index])
    turned = lax.all_to_all(
        (result * inv_root).astype(jnp.bfloat16).reshape(band_count, CH_DEV, 2, columns),
        "band",
        split_axis=0,
        concat_axis=0,
        tiled=True,
    )
    channel_major = turned.reshape(band_count, CH_DEV, 2, device_signals, spec_dev)
    channel_major = channel_major.transpose(1, 2, 4, 0, 3).reshape(
        CH_DEV, 2, spec_dev, band_count * device_signals
    )
    signal_index = (
        antenna_source_lookup[:, None] * polarization_count
        + jnp.arange(polarization_count, dtype=jnp.int32)[None, :]
    ).reshape(-1)
    channel_major = jnp.take(channel_major, signal_index, axis=3)
    total_sig = channel_major.shape[3]
    quarter_rows = total_sig // quarters
    start_row = lax.axis_index("quarter") * quarter_rows
    shard_piece = lax.all_gather(channel_major, "quarter", axis=2, tiled=True)
    own_rows = lax.dynamic_slice_in_dim(shard_piece, start_row, quarter_rows, 3)
    visibility = pair_product(left_side(own_rows), shard_piece)
    return (visibility * (1.0 / (spec_dev * quarters))).astype(jnp.bfloat16)


def solution(mesh):
    placed = (P("band", None, "quarter"), P("band"), P())
    return jax.shard_map(
        shards,
        mesh=mesh,
        in_specs=placed,
        out_specs=P(None, "band", "quarter", None),
        check_vma=False,
    )
```

profile of v0, /device:TPU:0, one launch (start us, length us, event | category | flops | bytes accessed | tf_op | source)
XLA Modules:
  0.0 57.7 jit_solution(4234828040600836542)
XLA Ops:
  0.0 0.6 %fusion.13 = f32[32768]{0:T(1024)S(1)} fusion(), kind=kLoop, calls=%fused_computation.34 | loop fusion | flops 1310720 | bytes 131072 | tf_op jit(solution)/shard_map/mul | solution.py:22
  0.6 0.7 %subtract_convert_fusion = bf16[4]{0:T(256)(128)(2,1)S(1)} fusion(s32[4]{0:T(128)} %param.4), kind=kLoop, calls=%fused_computation.67 | loop fusion | flops 8 | bytes 24 | tf_op jit(solution)/shard_map/convert_element_type | solution.py:59
  1.4 0.1 copy.41
  1.5 6.5 %multiply_convert_fusion.3 = (bf16[4,2,131072]{2,1,0:T(2,128)(2,1)}, bf16[4,2,131072]{2,1,0:T(2,128)(2,1)}) fusion(f32[131072]{0:T(1024)S(1)} %bitcast.47, bf16[4,2,131072]{2,1,0:T(2,128)(2,1)} %param.3, bf16[4]{0:T(256)(128)(2,1)S(1)} %subtract_convert_fusion), kind=kLoop, calls=%fused_computation.4 | loop fusion | flops 4194304 | bytes 6815752 | tf_op jit(solution)/shard_map/convert_element_type | solution.py:72
  8.0 0.0 copy-start.2
  8.0 3.6 %reshape.200 = bf16[8,16,8192]{2,1,0:T(8,128)(2,1)S(1)} reshape(bf16[4,2,131072]{2,1,0:T(2,128)(2,1)} %get-tuple-element.6) | data formatting | bytes 4194304 | tf_op jit(solution)/shard_map/reshape | solution.py:60
  11.5 0.0 copy-start.1
  11.6 1.1 %slice.56 = bf16[8,3,8192]{2,1,0:T(4,128)(2,1)} slice(bf16[8,16,8192]{2,1,0:T(8,128)(2,1)S(1)} %reshape.200), slice={[0:8], [0:3], [0:8192]} | slice | bytes 786432 | tf_op jit(solution)/shard_map/slice | solution.py:65
  12.7 1.3 %collective-permute-start = (bf16[8,3,8192]{2,1,0:T(4,128)(2,1)}, bf16[8,3,8192]{2,1,0:T(4,128)(2,1)}, u32[]{:S(2)}, u32[]{:S(2)}) collective-permute-start(bf16[8,3,8192]{2,1,0:T(4,128)(2,1)} %slice.56), channel_id=1, source_target_pairs={{1,0},{2,1},{3,2},{5,4},{6,5},{7,6},{9,8},{10,9},{11,10},{13,12},{... | collective-permute-start | bytes 1179656 | tf_op jit(solution)/shard_map/ppermute | solution.py:15
  14.0 0.0 copy-done.2
  14.0 0.1 iota_add_fusion
  14.1 0.1 add.219
  14.2 0.0 copy-done.1
  14.2 0.1 add.197
  14.3 1.7 %constant_dynamic-update-slice_fusion.1 = bf16[8,19,8192]{2,1,0:T(8,128)(2,1)S(1)} fusion(bf16[8,16,8192]{2,1,0:T(8,128)(2,1)} %copy-done.1), kind=kLoop, calls=%fused_computation.62 | loop fusion | bytes 4194304
  16.1 2.5 %cosine_convert_fusion = (bf16[16,1,8192]{2,0,1:T(8,128)(2,1)S(1)}, bf16[16,1,8192]{2,0,1:T(8,128)(2,1)S(1)}) fusion(s32[16]{0:T(128)S(1)} %iota_add_fusion.1), kind=kLoop, calls=%fused_computation.19 | loop fusion | flops 2228224 | bytes 524352 | tf_op jit(solution)/shard_map/convert
  18.5 0.1 pad_maximum_fusion
  18.6 1.4 %copy.27 = bf16[16,2,8192]{2,1,0:T(2,128)(2,1)} copy(bf16[16,2,8192]{2,0,1:T(8,128)(2,1)S(1)} %pad_maximum_fusion) | data formatting | bytes 1048576 | tf_op jit(solution)/shard_map/stack | solution.py:30
  20.0 2.1 %convert_element_type.86 = bf16[32,8192]{1,0:T(8,128)(2,1)} reshape(bf16[16,2,8192]{2,1,0:T(2,128)(2,1)} %copy.27) | data formatting | bytes 1048576 | tf_op jit(solution)/shard_map/convert_element_type | solution.py:31
  22.0 4.7 %convert_element_type.90 = bf16[128,8192]{1,0:T(8,128)(2,1)} reshape(bf16[4,2,131072]{2,1,0:T(2,128)(2,1)} %get-tuple-element.5) | data formatting | bytes 4194304 | tf_op jit(solution)/shard_map/convert_element_type | solution.py:72
  26.7 2.6 %fusion.32 = f32[32,128]{1,0:T(8,128)S(1)} fusion(bf16[32,8192]{1,0:T(8,128)(2,1)} %convert_element_type.86, bf16[128,8192]{1,0:T(8,128)(2,1)} %convert_element_type.90), kind=kOutput, calls=%fused_computation.76 | convolution fusion | flops 67108864 | bytes 2637824 | tf_op jit(solution)/shard_map/dot_general | solution.py:48
  29.3 0.0 collective-permute-done
  29.3 1.4 %constant_dynamic-update-slice_fusion = bf16[8,19,8192]{2,1,0:T(8,128)(2,1)S(1)} fusion(bf16[8,19,8192]{2,1,0:T(8,128)(2,1)S(1)} %constant_dynamic-update-slice_fusion.1, bf16[8,3,8192]{2,1,0:T(4,128)(2,1)} %collective-permute-done), kind=kLoop, calls=%fused_computation.61 | loop fusion | bytes 917504 | tf_op jit(solution)/shard_map/concatenate | solution.py:66
  30.7 0.0 copy-start
  30.7 1.8 %multiply_convert_fusion.1 = (bf16[8,16,8192]{2,1,0:T(8,128)(2,1)S(1)}, bf16[8,16,8192]{2,1,0:T(8,128)(2,1)S(1)}, bf16[8,16,8192]{2,1,0:T(8,128)(2,1)S(1)}) fusion(bf16[8,19,8192]{2,1,0:T(8,128)(2,1)S(1)} %constant_dynamic-update-slice_fusion, f32[8192]{0:T(1024)S(1)} %get-tuple-element.10, f32[8192]{0:T(1024)S(1)} %get-tuple-element.11, ...), kind=kLoop, calls=%fused_computation.2 | loop fusion | flops 9437184 | bytes 12681216 | tf_op jit(solution)/shard_map/convert_element_type | solution.py:72
  32.5 0.0 copy-done
  32.5 0.8 %fusion.33 = f32[32,128]{1,0:T(8,128)S(1)} fusion(bf16[32,8192]{1,0:T(8,128)(2,1)S(1)} %copy-done, bf16[128,8192]{1,0:T(8,128)(2,1)S(1)} %bitcast.44), kind=kOutput, calls=%fused_computation.77 | convolution fusion | flops 67108864 | bytes 2637824 | tf_op jit(solution)/shard_map/dot_general | solution.py:48
  33.3 0.8 %convolution_add_fusion.1 = f32[32,128]{1,0:T(8,128)S(1)} fusion(f32[32,128]{1,0:T(8,128)S(1)} %fusion.32, bf16[32,8192]{1,0:T(8,128)(2,1)S(1)} %copy-done, bf16[128,8192]{1,0:T(8,128)(2,1)S(1)} %bitcast.46), kind=kOutput, calls=%fused_computation.8 | convolution fusion | flops 67112960 | bytes 2654208 | tf_op jit(solution)/shard_map/dot_general | solution.py:48
  34.2 1.4 %fusion.2 = bf16[32,128]{1,0:T(8,128)(2,1)} fusion(f32[32,128]{1,0:T(8,128)S(1)} %fusion.33, f32[32,128]{1,0:T(8,128)S(1)} %convolution_add_fusion.1, bf16[32,8192]{1,0:T(8,128)(2,1)S(1)} %copy-done, bf16[128,8192]{1,0:T(8,128)(2,1)S(1)} %bitcast.45), kind=kOutput, calls=%fused_computation.9 | convolution fusion | flops 67125248 | bytes 2662400 | tf_op jit(solution)/shard_map/dot_general | solution.py:48
  35.6 7.3 %all-to-all-start = ((bf16[8,2,2,128]{3,2,1,0:T(2,128)(2,1)}), bf16[8,2,2,128]{3,2,1,0:T(2,128)(2,1)S(1)}, u32[]{:S(2)}, u32[]{:S(2)}) async-start(bf16[8,2,2,128]{3,2,1,0:T(2,128)(2,1)} %bitcast.3), calls=%async_computation | async-start | bytes 16384 | tf_op jit(solution)/shard_map/all_to_all | solution.py:78
  42.9 6.5 %all-to-all-done = bf16[8,2,2,128]{3,2,1,0:T(2,128)(2,1)S(1)} async-done(((bf16[8,2,2,128]{3,2,1,0:T(2,128)(2,1)}), bf16[8,2,2,128]{3,2,1,0:T(2,128)(2,1)S(1)}, u32[]{:S(2)}, u32[]{:S(2)}) %all-to-all-start) | async-done | bytes 8224 | tf_op jit(solution)/shard_map/all_to_all | solution.py:78
  49.4 0.1 reshape.205
  49.5 0.1 copy.29
  49.6 0.7 %gather_fusion = bf16[64,2,2,16]{3,2,1,0:T(2,128)(2,1)S(1)} fusion(bf16[2,2,16,64]{2,1,3,0:T(2,128)(2,1)S(1)} %copy.29, s32[1024]{0:T(1024)S(1)} %pad_clamp_fusion), kind=kCustom, calls=%fused_computation | custom fusion | bytes 16640 | tf_op jit(solution)/shard_map/jit(_take)/gather | solution.py:93
  50.3 0.1 fusion.22
  50.5 0.1 copy.30
  50.6 5.5 %all_gather.3 = bf16[2,2,64,64]{3,1,0,2:T(2,128)(2,1)S(1)} all-gather(bf16[2,2,16,64]{3,1,0,2:T(2,128)(2,1)S(1)} %copy.30), channel_id=1, replica_groups=mesh['band'=8,'quarter'=4] {'quarter'}, dimensions={2}, use_global_device_ids=true | all-gather | bytes 40960 | tf_op jit(solution)/shard_map/all_gather | solution.py:97
  56.1 0.1 fusion.31
  56.2 0.2 constant_dynamic-slice_fusion.1
  56.4 0.1 copy.40
  56.5 0.1 copy.39
  56.6 0.1 copy.36
  56.7 0.1 copy.37
  56.8 0.1 maximum_bitcast_fusion
  56.9 0.2 fusion.23
  57.1 0.6 %copy.35 = bf16[2,2,16,64]{3,2,1,0:T(8,128)(2,1)} copy(bf16[2,2,16,64]{3,2,0,1:T(8,128)(2,1)S(1)} %fusion.27) | data formatting | bytes 16384 | tf_op jit(solution)/shard_map/convert_element_type | solution.py:100
  (11 shorter events, 0.1 us)
Async XLA Ops:
  8.0 6.0 %copy-start.2 = (s32[32]{0:T(128)S(1)}, s32[32]{0:T(128)}, u32[]{:S(2)}) copy-start(s32[32]{0:T(128)} %param.5) | copy-start | bytes 388
  11.5 2.6 %copy-start.1 = (bf16[8,16,8192]{2,1,0:T(8,128)(2,1)}, bf16[8,16,8192]{2,1,0:T(8,128)(2,1)S(1)}, u32[]{:S(2)}) copy-start(bf16[8,16,8192]{2,1,0:T(8,128)(2,1)S(1)} %reshape.200) | copy-start | bytes 6291460
  12.7 16.6 %collective-permute-start = (bf16[8,3,8192]{2,1,0:T(4,128)(2,1)}, bf16[8,3,8192]{2,1,0:T(4,128)(2,1)}, u32[]{:S(2)}, u32[]{:S(2)}) collective-permute-start(bf16[8,3,8192]{2,1,0:T(4,128)(2,1)} %slice.56), channel_id=1, source_target_pairs={{1,0},{2,1},{3,2},{5,4},{6,5},{7,6},{9,8},{10,9},{11,10},{13,12},{... | collective-permute-start | bytes 1179656 | tf_op jit(solution)/shard_map/ppermute | solution.py:15
  30.7 1.8 %copy-start = (bf16[32,8192]{1,0:T(8,128)(2,1)S(1)}, bf16[32,8192]{1,0:T(8,128)(2,1)}, u32[]{:S(2)}) copy-start(bf16[32,8192]{1,0:T(8,128)(2,1)} %convert_element_type.86) | copy-start | bytes 1572868
  35.6 13.8 %all-to-all-start = ((bf16[8,2,2,128]{3,2,1,0:T(2,128)(2,1)}), bf16[8,2,2,128]{3,2,1,0:T(2,128)(2,1)S(1)}, u32[]{:S(2)}, u32[]{:S(2)}) async-start(bf16[8,2,2,128]{3,2,1,0:T(2,128)(2,1)} %bitcast.3), calls=%async_computation | async-start | bytes 16384 | tf_op jit(solution)/shard_map/all_to_all | solution.py:78
where the time goes:
time: 58.2 us; the launch traced here: 57.7 us
  local copies, waits for them, and re-layouts  18.6 us (32%)
  other arithmetic  12.5 us (21%)
  starting transfers between devices  8.56 us (15%)
  waiting for transfers between devices  6.53 us (11%)
  matrix products  5.84 us (10%)
  blocking collectives  5.48 us (9%)
    convert_element_type x2, other arithmetic, shards(): tap_win = (window[tap_index] * extended[:, tap_index:tap_index + spec_dev...  8.3 us
    all_to_all x1, starting transfers between devices, shards(): lax.all_to_all((result * inv_root).astype(jnp.bfloat16).reshape(band_coun...  7.28 us
    all_to_all x1, waiting for transfers between devices, shards(): lax.all_to_all((result * inv_root).astype(jnp.bfloat16).reshape(band_coun...  6.51 us
    dot_general x4, matrix products, table_product(): lax.dot_general(table_rows, windowed_rows, (((1,), (1,)), ((), ())), pref...  5.63 us
    all_gather x1, blocking collectives, shards(): shard_piece = lax.all_gather(channel_major, 'quarter', axis=2, tiled=True)  5.48 us
    convert_element_type x1, local copies, waits for them, and re-layouts, shards(): tap_win = (window[tap_index] * extended[:, tap_index:tap_index + spec_dev...  4.67 us
    reshape x1, local copies, waits for them, and re-layouts, shards(): (voltages * keep_mask[:, None, None]).reshape(device_signals, spec_dev, F...  3.58 us
    another operation x1, other arithmetic  2.47 us
  transfers between devices with their start and end apart: 2, of which 1 were waited for; matrix products, arithmetic and copies ran while one was open for 26% of the time, Pallas kernels for 0%

commit v1 on v0

--- a/solution.py
+++ b/solution.py
@@ -94,7 +94,14 @@
     total_sig = channel_major.shape[3]
     quarter_rows = total_sig // quarters
     start_row = lax.axis_index("quarter") * quarter_rows
-    shard_piece = lax.all_gather(channel_major, "quarter", axis=2, tiled=True)
+    ring = [channel_major]
+    for hop in range(3):
+        ring.append(lax.ppermute(ring[-1], "quarter", [(dev, (dev + 1) % 4) for dev in range(4)]))
+    shard_piece = jnp.roll(
+        jnp.concatenate(ring[::-1], axis=2),
+        (lax.axis_index("quarter") + 1) * ring[0].shape[2],
+        axis=2,
+    )
     own_rows = lax.dynamic_slice_in_dim(shard_piece, start_row, quarter_rows, 3)
     visibility = pair_product(left_side(own_rows), shard_piece)
     return (visibility * (1.0 / (spec_dev * quarters))).astype(jnp.bfloat16)

time: 58.2 us -> 63.6 us (1.093)
  waiting for transfers between devices: 6.53 us -> 17.7 us
  blocking collectives: 5.48 us -> 0 us
    ppermute x0 -> x3, waiting for transfers between devices: none -> 11.2 us  [shards(): lax.ppermute(ring[-1], 'quarter', [(dev, (dev + 1) % 4) for dev in range(...]
    all_gather x1 -> x0, blocking collectives: 5.48 us -> none  [shards(): shard_piece = lax.all_gather(channel_major, 'quarter', axis=2, tiled=True)]
    unnamed x13 -> x9, local copies, waits for them, and re-layouts: 2.26 us -> 1.88 us
  transfers between devices with their start and end apart: 2 -> 5, of which waited for: 1 -> 4; matrix products, arithmetic and copies ran while one was open for 26% -> 24% of each run, Pallas kernels for 0% -> 0%
where the time goes in v1:
time: 63.6 us; the launch traced here: 63.1 us
  local copies, waits for them, and re-layouts  18.2 us (29%)
  waiting for transfers between devices  17.7 us (28%)
  other arithmetic  12.5 us (20%)
  starting transfers between devices  8.62 us (14%)
  matrix products  5.84 us (9%)
    ppermute x3, waiting for transfers between devices, shards(): lax.ppermute(ring[-1], 'quarter', [(dev, (dev + 1) % 4) for dev in range(...  11.2 us
    convert_element_type x2, other arithmetic, shards(): tap_win = (window[tap_index] * extended[:, tap_index:tap_index + spec_dev...  8.31 us
    all_to_all x1, starting transfers between devices, shards(): lax.all_to_all((result * inv_root).astype(jnp.bfloat16).reshape(band_coun...  7.28 us
    all_to_all x1, waiting for transfers between devices, shards(): lax.all_to_all((result * inv_root).astype(jnp.bfloat16).reshape(band_coun...  6.51 us
    dot_general x4, matrix products, table_product(): lax.dot_general(table_rows, windowed_rows, (((1,), (1,)), ((), ())), pref...  5.63 us
    convert_element_type x1, local copies, waits for them, and re-layouts, shards(): tap_win = (window[tap_index] * extended[:, tap_index:tap_index + spec_dev...  4.67 us
    reshape x1, local copies, waits for them, and re-layouts, shards(): (voltages * keep_mask[:, None, None]).reshape(device_signals, spec_dev, F...  3.58 us
    another operation x1, other arithmetic  2.47 us
  transfers between devices with their start and end apart: 5, of which 4 were waited for; matrix products, arithmetic and copies ran while one was open for 24% of the time, Pallas kernels for 0%

profile of v1, /device:TPU:0, one launch (start us, length us, event | category | flops | bytes accessed | tf_op | source)
XLA Modules:
  0.0 63.1 jit_solution(12591098626278428405)
XLA Ops:
  0.0 0.6 %fusion.13 = f32[32768]{0:T(1024)S(1)} fusion(), kind=kLoop, calls=%fused_computation.34 | loop fusion | flops 1310720 | bytes 131072 | tf_op jit(solution)/shard_map/mul | solution.py:22
  0.6 0.7 %subtract_convert_fusion = bf16[4]{0:T(256)(128)(2,1)S(1)} fusion(s32[4]{0:T(128)} %param.4), kind=kLoop, calls=%fused_computation.71 | loop fusion | flops 8 | bytes 24 | tf_op jit(solution)/shard_map/convert_element_type | solution.py:59
  1.4 0.1 copy.22
  1.5 6.5 %multiply_convert_fusion.3 = (bf16[4,2,131072]{2,1,0:T(2,128)(2,1)}, bf16[4,2,131072]{2,1,0:T(2,128)(2,1)}) fusion(f32[131072]{0:T(1024)S(1)} %bitcast.51, bf16[4,2,131072]{2,1,0:T(2,128)(2,1)} %param.3, bf16[4]{0:T(256)(128)(2,1)S(1)} %subtract_convert_fusion), kind=kLoop, calls=%fused_computation.4 | loop fusion | flops 4194304 | bytes 6815752 | tf_op jit(solution)/shard_map/convert_element_type | solution.py:72
  8.0 0.0 copy-start.2
  8.0 3.6 %reshape.200 = bf16[8,16,8192]{2,1,0:T(8,128)(2,1)S(1)} reshape(bf16[4,2,131072]{2,1,0:T(2,128)(2,1)} %get-tuple-element.8) | data formatting | bytes 4194304 | tf_op jit(solution)/shard_map/reshape | solution.py:60
  11.5 0.0 copy-start.1
  11.6 1.1 %slice.56 = bf16[8,3,8192]{2,1,0:T(4,128)(2,1)} slice(bf16[8,16,8192]{2,1,0:T(8,128)(2,1)S(1)} %reshape.200), slice={[0:8], [0:3], [0:8192]} | slice | bytes 786432 | tf_op jit(solution)/shard_map/slice | solution.py:65
  12.7 1.3 %collective-permute-start = (bf16[8,3,8192]{2,1,0:T(4,128)(2,1)}, bf16[8,3,8192]{2,1,0:T(4,128)(2,1)}, u32[]{:S(2)}, u32[]{:S(2)}) collective-permute-start(bf16[8,3,8192]{2,1,0:T(4,128)(2,1)} %slice.56), channel_id=1, source_target_pairs={{1,0},{2,1},{3,2},{5,4},{6,5},{7,6},{9,8},{10,9},{11,10},{13,12},{... | collective-permute-start | bytes 1179656 | tf_op jit(solution)/shard_map/ppermute | solution.py:15
  14.0 0.0 copy-done.2
  14.0 0.1 iota_add_fusion
  14.1 0.1 add.236
  14.2 0.0 copy-done.1
  14.2 0.1 add.214
  14.3 1.7 %constant_dynamic-update-slice_fusion.1 = bf16[8,19,8192]{2,1,0:T(8,128)(2,1)S(1)} fusion(bf16[8,16,8192]{2,1,0:T(8,128)(2,1)} %copy-done.1), kind=kLoop, calls=%fused_computation.66 | loop fusion | bytes 4194304
  16.0 2.5 %cosine_convert_fusion = (bf16[16,1,8192]{2,0,1:T(8,128)(2,1)S(1)}, bf16[16,1,8192]{2,0,1:T(8,128)(2,1)S(1)}) fusion(s32[16]{0:T(128)S(1)} %iota_add_fusion.1), kind=kLoop, calls=%fused_computation.19 | loop fusion | flops 2228224 | bytes 524352 | tf_op jit(solution)/shard_map/convert
  18.5 0.1 pad_maximum_fusion
  18.6 1.3 %copy.16 = bf16[16,2,8192]{2,1,0:T(2,128)(2,1)} copy(bf16[16,2,8192]{2,0,1:T(8,128)(2,1)S(1)} %pad_maximum_fusion) | data formatting | bytes 1048576 | tf_op jit(solution)/shard_map/stack | solution.py:30
  19.9 2.1 %convert_element_type.86 = bf16[32,8192]{1,0:T(8,128)(2,1)} reshape(bf16[16,2,8192]{2,1,0:T(2,128)(2,1)} %copy.16) | data formatting | bytes 1048576 | tf_op jit(solution)/shard_map/convert_element_type | solution.py:31
  22.0 4.7 %convert_element_type.90 = bf16[128,8192]{1,0:T(8,128)(2,1)} reshape(bf16[4,2,131072]{2,1,0:T(2,128)(2,1)} %get-tuple-element.7) | data formatting | bytes 4194304 | tf_op jit(solution)/shard_map/convert_element_type | solution.py:72
  26.7 2.6 %fusion.32 = f32[32,128]{1,0:T(8,128)S(1)} fusion(bf16[32,8192]{1,0:T(8,128)(2,1)} %convert_element_type.86, bf16[128,8192]{1,0:T(8,128)(2,1)} %convert_element_type.90), kind=kOutput, calls=%fused_computation.77 | convolution fusion | flops 67108864 | bytes 2637824 | tf_op jit(solution)/shard_map/dot_general | solution.py:48
  29.2 0.0 collective-permute-done
  29.2 1.4 %constant_dynamic-update-slice_fusion = bf16[8,19,8192]{2,1,0:T(8,128)(2,1)S(1)} fusion(bf16[8,19,8192]{2,1,0:T(8,128)(2,1)S(1)} %constant_dynamic-update-slice_fusion.1, bf16[8,3,8192]{2,1,0:T(4,128)(2,1)} %collective-permute-done), kind=kLoop, calls=%fused_computation.65 | loop fusion | bytes 917504 | tf_op jit(solution)/shard_map/concatenate | solution.py:66
  30.7 0.0 copy-start
  30.7 1.8 %multiply_convert_fusion.1 = (bf16[8,16,8192]{2,1,0:T(8,128)(2,1)S(1)}, bf16[8,16,8192]{2,1,0:T(8,128)(2,1)S(1)}, bf16[8,16,8192]{2,1,0:T(8,128)(2,1)S(1)}) fusion(bf16[8,19,8192]{2,1,0:T(8,128)(2,1)S(1)} %constant_dynamic-update-slice_fusion, f32[8192]{0:T(1024)S(1)} %get-tuple-element.12, f32[8192]{0:T(1024)S(1)} %get-tuple-element.13, ...), kind=kLoop, calls=%fused_computation.2 | loop fusion | flops 9437184 | bytes 12681216 | tf_op jit(solution)/shard_map/convert_element_type | solution.py:72
  32.5 0.0 copy-done
  32.5 0.8 %fusion.33 = f32[32,128]{1,0:T(8,128)S(1)} fusion(bf16[32,8192]{1,0:T(8,128)(2,1)S(1)} %copy-done, bf16[128,8192]{1,0:T(8,128)(2,1)S(1)} %bitcast.48), kind=kOutput, calls=%fused_computation.78 | convolution fusion | flops 67108864 | bytes 2637824 | tf_op jit(solution)/shard_map/dot_general | solution.py:48
  33.3 0.8 %convolution_add_fusion.1 = f32[32,128]{1,0:T(8,128)S(1)} fusion(f32[32,128]{1,0:T(8,128)S(1)} %fusion.32, bf16[32,8192]{1,0:T(8,128)(2,1)S(1)} %copy-done, bf16[128,8192]{1,0:T(8,128)(2,1)S(1)} %bitcast.50), kind=kOutput, calls=%fused_computation.8 | convolution fusion | flops 67112960 | bytes 2654208 | tf_op jit(solution)/shard_map/dot_general | solution.py:48
  34.1 1.4 %fusion.2 = bf16[32,128]{1,0:T(8,128)(2,1)} fusion(f32[32,128]{1,0:T(8,128)S(1)} %fusion.33, f32[32,128]{1,0:T(8,128)S(1)} %convolution_add_fusion.1, bf16[32,8192]{1,0:T(8,128)(2,1)S(1)} %copy-done, bf16[128,8192]{1,0:T(8,128)(2,1)S(1)} %bitcast.49), kind=kOutput, calls=%fused_computation.9 | convolution fusion | flops 67125248 | bytes 2662400 | tf_op jit(solution)/shard_map/dot_general | solution.py:48
  35.6 7.3 %all-to-all-start = ((bf16[8,2,2,128]{3,2,1,0:T(2,128)(2,1)}), bf16[8,2,2,128]{3,2,1,0:T(2,128)(2,1)S(1)}, u32[]{:S(2)}, u32[]{:S(2)}) async-start(bf16[8,2,2,128]{3,2,1,0:T(2,128)(2,1)} %bitcast.3), calls=%async_computation | async-start | bytes 16384 | tf_op jit(solution)/shard_map/all_to_all | solution.py:78
  42.9 6.5 %all-to-all-done = bf16[8,2,2,128]{3,2,1,0:T(2,128)(2,1)S(1)} async-done(((bf16[8,2,2,128]{3,2,1,0:T(2,128)(2,1)}), bf16[8,2,2,128]{3,2,1,0:T(2,128)(2,1)S(1)}, u32[]{:S(2)}, u32[]{:S(2)}) %all-to-all-start) | async-done | bytes 8224 | tf_op jit(solution)/shard_map/all_to_all | solution.py:78
  49.4 0.1 reshape.205
  49.5 0.1 copy.18
  49.6 0.7 %gather_fusion = bf16[64,2,2,16]{3,2,1,0:T(2,128)(2,1)S(1)} fusion(bf16[2,2,16,64]{2,1,3,0:T(2,128)(2,1)S(1)} %copy.18, s32[1024]{0:T(1024)S(1)} %pad_clamp_fusion), kind=kCustom, calls=%fused_computation | custom fusion | bytes 16640 | tf_op jit(solution)/shard_map/jit(_take)/gather | solution.py:93
  50.3 0.1 fusion.22
  50.4 0.1 collective-permute-start.1
  50.4 3.8 %collective-permute-done.1 = bf16[2,2,16,64]{2,3,0,1:T(8,128)(2,1)S(1)} collective-permute-done((bf16[2,2,16,64]{2,3,0,1:T(8,128)(2,1)S(1)}, bf16[2,2,16,64]{2,3,0,1:T(8,128)(2,1)S(1)}, u32[]{:S(2)}, u32[]{:S(2)}) %collective-permute-start.1) | collective-permute-done | bytes 8224 | tf_op jit(solution)/shard_map/ppermute | solution.py:99
  54.3 0.0 collective-permute-start.2
  54.3 3.7 %collective-permute-done.2 = bf16[2,2,16,64]{2,3,0,1:T(8,128)(2,1)S(1)} collective-permute-done((bf16[2,2,16,64]{2,3,0,1:T(8,128)(2,1)S(1)}, bf16[2,2,16,64]{2,3,0,1:T(8,128)(2,1)S(1)}, u32[]{:S(2)}, u32[]{:S(2)}) %collective-permute-start.2) | collective-permute-done | bytes 8224 | tf_op jit(solution)/shard_map/ppermute | solution.py:99
  58.0 0.0 collective-permute-start.3
  58.0 3.7 %collective-permute-done.3 = bf16[2,2,16,64]{2,3,0,1:T(8,128)(2,1)S(1)} collective-permute-done((bf16[2,2,16,64]{2,3,0,1:T(8,128)(2,1)S(1)}, bf16[2,2,16,64]{2,3,0,1:T(8,128)(2,1)S(1)}, u32[]{:S(2)}, u32[]{:S(2)}) %collective-permute-start.3) | collective-permute-done | bytes 8224 | tf_op jit(solution)/shard_map/ppermute | solution.py:99
  61.6 0.2 concatenate.19
  61.9 0.1 fusion.30
  62.0 0.1 dynamic-slice_bitcast_fusion.2
  62.0 0.1 dynamic-slice_bitcast_fusion.1
  62.1 0.1 maximum_bitcast_fusion
  62.2 0.2 fusion.23
  62.5 0.6 copy.21
  (10 shorter events, 0.1 us)
Async XLA Ops:
  8.0 6.0 %copy-start.2 = (s32[32]{0:T(128)S(1)}, s32[32]{0:T(128)}, u32[]{:S(2)}) copy-start(s32[32]{0:T(128)} %param.5) | copy-start | bytes 388
  11.5 2.6 %copy-start.1 = (bf16[8,16,8192]{2,1,0:T(8,128)(2,1)}, bf16[8,16,8192]{2,1,0:T(8,128)(2,1)S(1)}, u32[]{:S(2)}) copy-start(bf16[8,16,8192]{2,1,0:T(8,128)(2,1)S(1)} %reshape.200) | copy-start | bytes 6291460
  12.7 16.6 %collective-permute-start = (bf16[8,3,8192]{2,1,0:T(4,128)(2,1)}, bf16[8,3,8192]{2,1,0:T(4,128)(2,1)}, u32[]{:S(2)}, u32[]{:S(2)}) collective-permute-start(bf16[8,3,8192]{2,1,0:T(4,128)(2,1)} %slice.56), channel_id=1, source_target_pairs={{1,0},{2,1},{3,2},{5,4},{6,5},{7,6},{9,8},{10,9},{11,10},{13,12},{... | collective-permute-start | bytes 1179656 | tf_op jit(solution)/shard_map/ppermute | solution.py:15
  30.7 1.8 %copy-start = (bf16[32,8192]{1,0:T(8,128)(2,1)S(1)}, bf16[32,8192]{1,0:T(8,128)(2,1)}, u32[]{:S(2)}) copy-start(bf16[32,8192]{1,0:T(8,128)(2,1)} %convert_element_type.86) | copy-start | bytes 1572868
  35.6 13.8 %all-to-all-start = ((bf16[8,2,2,128]{3,2,1,0:T(2,128)(2,1)}), bf16[8,2,2,128]{3,2,1,0:T(2,128)(2,1)S(1)}, u32[]{:S(2)}, u32[]{:S(2)}) async-start(bf16[8,2,2,128]{3,2,1,0:T(2,128)(2,1)} %bitcast.3), calls=%async_computation | async-start | bytes 16384 | tf_op jit(solution)/shard_map/all_to_all | solution.py:78
  50.4 3.9 %collective-permute-start.1 = (bf16[2,2,16,64]{2,3,0,1:T(8,128)(2,1)S(1)}, bf16[2,2,16,64]{2,3,0,1:T(8,128)(2,1)S(1)}, u32[]{:S(2)}, u32[]{:S(2)}) collective-permute-start(bf16[2,2,16,64]{2,3,0,1:T(8,128)(2,1)S(1)} %fusion.22), channel_id=1, source_target_pairs={{0,1},{1,2},{2,3},{3,0},{4,5},{5,6},{6,7},{7,4},{8,9},{9,10},{10,1... | collective-permute-start | bytes 24584 | tf_op jit(solution)/shard_map/ppermute | solution.py:99
  54.3 3.7 %collective-permute-start.2 = (bf16[2,2,16,64]{2,3,0,1:T(8,128)(2,1)S(1)}, bf16[2,2,16,64]{2,3,0,1:T(8,128)(2,1)S(1)}, u32[]{:S(2)}, u32[]{:S(2)}) collective-permute-start(bf16[2,2,16,64]{2,3,0,1:T(8,128)(2,1)S(1)} %collective-permute-done.1), channel_id=1, source_target_pairs={{0,1},{1,2},{2,3},{3,0},{4,5},{5,6},{6,7},{7,4},{8,9},{9,10},{10,1... | collective-permute-start | bytes 24584 | tf_op jit(solution)/shard_map/ppermute | solution.py:99
  58.0 3.7 %collective-permute-start.3 = (bf16[2,2,16,64]{2,3,0,1:T(8,128)(2,1)S(1)}, bf16[2,2,16,64]{2,3,0,1:T(8,128)(2,1)S(1)}, u32[]{:S(2)}, u32[]{:S(2)}) collective-permute-start(bf16[2,2,16,64]{2,3,0,1:T(8,128)(2,1)S(1)} %collective-permute-done.2), channel_id=1, source_target_pairs={{0,1},{1,2},{2,3},{3,0},{4,5},{5,6},{6,7},{7,4},{8,9},{9,10},{10,1... | collective-permute-start | bytes 24584 | tf_op jit(solution)/shard_map/ppermute | solution.py:99
